TPU v7x, 32 devices: a whole 2x2x4 slice. The times are simulated.
32 devices in a mesh: band: 32 (over z, y, x, core).
Axes of the slice: x: 2, y: 2, z: 4, core: 2. Of those that a mesh axis runs over, the one named last changes fastest.
Arguments:
- rho_low: float32 [2, 32, 128, 128], replicated, may hold values from -6 to 6
- kprev_low: float32 [2, 32, 128, 128], replicated, may hold values from -6 to 6
- rho_band: float32 [2, 512, 128, 128], P(None, 'band'), may hold values from -6 to 6
- kprev_band: float32 [2, 512, 128, 128], P(None, 'band'), may hold values from -6 to 6
- hamiltonian: float32 [2, 128, 128], replicated, as said below
- state_site: int32 [128], replicated, may hold values from 0 to 23
- coupling_mag: float32 [72], replicated, may hold values from 0.2 to 2
- coupling_phase: float32 [72], replicated, may hold values from -3.140625 to 3.140625
- damping_rate: float32 [72], replicated, may hold values from 0.05 to 2
- low_mode: int32 [31], replicated, may hold values from 0 to 71, as said below
- occupation: int32 [512, 72], P('band'), may hold values from 0 to 3, as said below
- couple_src: int32 [512, 16], P('band'), may hold values from -1 to 543, as said below
- couple_mode: int32 [512, 16], P('band'), may hold values from 0 to 71, as said below
- couple_dir: int32 [512, 16], P('band'), may hold values from 0 to 1
Outputs:
- k_low: float32 [2, 32, 128, 128], replicated
- k_band: float32 [2, 512, 128, 128], P(None, 'band')
Inputs may be any that keep to these rules, and one draw needn't show every extreme that they name: `hamiltonian`: the real part is symmetric and the imaginary part antisymmetric (a Hermitian matrix). `low_mode`: distinct modes. `occupation`: each operator has one to three quanta in all. `couple_src`: all couplings of one device's operators to operators held by one other device read one and the same operator of that device. A low-tier source is never 0, and couplings to low-tier sources have direction 1. Each device's far couplings reach devices spread over the whole axis. `couple_mode`: for direction 1 the mode is occupied in the destination operator.
All inputs are finite; a program needn't handle non-finite values.
Results may differ from a plain program's by a relative error of at most 0.0003.
Values sent between devices are 32-bit elements; how exact they have to be, the bound alone decides.
No kernel may reach another device: no remote copies, remote signals or barrier semaphores. Data moves between devices by JAX's collectives and lax.ppermute only.
A program may use at most 192 MiB of HBM per device.

v0:
```python
import jax
import jax.numpy as jnp
from jax import lax
from jax.sharding import PartitionSpec as P

EXPS = 3


section_weight = 0.2
highest = lax.Precision.HIGHEST


def commutator(ham, field):
    h_real, h_imag = (ham[0], ham[1])
    y_real, y_imag = (field[0], field[1])

    def left_mul(matrix, block):
        return jnp.einsum("ac,jcb->jab", matrix, block, precision=highest)

    def right_mul(block, matrix):
        return jnp.einsum("jac,cb->jab", block, matrix, precision=highest)

    comm_real = (
        left_mul(h_real, y_real)
        - left_mul(h_imag, y_imag)
        - right_mul(y_real, h_real)
        + right_mul(y_imag, h_imag)
    )
    comm_imag = (
        left_mul(h_real, y_imag)
        + left_mul(h_imag, y_real)
        - right_mul(y_real, h_imag)
        - right_mul(y_imag, h_real)
    )
    return jnp.stack([comm_imag, -comm_real])


def couple_term(source, site_rows, alpha_col, beta_col):
    diff_mask = site_rows[:, :, None] - site_rows[:, None, :]
    sum_mask = site_rows[:, :, None] + site_rows[:, None, :]
    real_part = alpha_col[:, None, None] * diff_mask
    imag_part = beta_col[:, None, None] * sum_mask
    x_real = real_part * source[0] - imag_part * source[1]
    x_imag = real_part * source[1] + imag_part * source[0]
    return jnp.stack([x_imag, -x_real])


def site_masks(state_site, modes):
    owner_site = jnp.arange(modes, dtype=jnp.int32) // EXPS
    return (state_site[None, :] == owner_site[:, None]).astype(jnp.float32)


def low_rest(y_low, site_mask, coupling_mag, coupling_phase, damping_rate, low_mode):
    others = y_low.shape[1] - 1
    site_rows = site_mask[low_mode]
    strength = jnp.sqrt(coupling_mag[low_mode])
    phase_col = coupling_phase[low_mode]
    upward = couple_term(y_low[:, 1:], site_rows, strength, jnp.zeros_like(strength))
    top_term = jnp.sum(upward, axis=1, keepdims=True)
    ground = jnp.broadcast_to(y_low[:, 0:1], (2, others) + y_low.shape[2:])
    downward = couple_term(
        ground, site_rows, strength * jnp.cos(phase_col), strength * jnp.sin(phase_col)
    )
    damping = jnp.concatenate([jnp.zeros((1,), jnp.float32), damping_rate[low_mode]])
    return jnp.concatenate([top_term, downward], axis=1) - damping[None, :, None, None] * y_low


def band_block(
    y_blk,
    position,
    source,
    mode,
    direction,
    occupation,
    source_pool,
    ham,
    site_mask,
    coupling_mag,
    coupling_phase,
    damping_rate,
    low_mode,
    low_partial,
):
    low_count = low_partial.shape[1]
    occ_float = occupation.astype(jnp.float32)
    damping = jnp.dot(occ_float, damping_rate, precision=highest)
    total = commutator(ham, y_blk) - damping[None, :, None, None] * y_blk
    low_marks = jnp.concatenate([jnp.full((1,), -1, jnp.int32), low_mode])

    def column(col_id, state_pair):
        total, low_partial = state_pair
        source_col = source[:, col_id]
        mode_col = mode[:, col_id]
        is_down = direction[:, col_id] == 1
        is_live = (source_col >= 0).astype(jnp.float32)
        occ_level = jnp.take_along_axis(occ_float, mode_col[:, None], axis=1)[:, 0]
        strength = coupling_mag[mode_col]
        phase_col = coupling_phase[mode_col]
        amp_up = jnp.sqrt((occ_level + 1.0) * strength)
        amp_down = jnp.sqrt(occ_level * strength)
        alpha_col = jnp.where(is_down, amp_down * jnp.cos(phase_col), amp_up) * is_live
        beta_col = jnp.where(is_down, amp_down * jnp.sin(phase_col), 0.0) * is_live
        site_rows = site_mask[mode_col]
        fetched = jnp.take(source_pool, position[:, col_id], axis=1)
        total = total + couple_term(fetched, site_rows, alpha_col, beta_col)
        is_low = ((source_col >= 0) & (source_col < low_count)).astype(jnp.float32)
        target = jnp.clip(source_col, 0, low_count - 1)
        held_mode = (low_marks[target] == mode_col).astype(jnp.float32)
        alpha_low = jnp.sqrt((held_mode + 1.0) * strength) * is_low
        back_term = couple_term(y_blk, site_rows, alpha_low, jnp.zeros_like(alpha_low))
        low_partial = low_partial.at[:, target].add(back_term)
        return (total, low_partial)

    return lax.fori_loop(0, source.shape[1], column, (total, low_partial))


def select_ados(y_band, asked_for):
    local_count = y_band.shape[1]
    chosen = jnp.take(y_band, jnp.clip(asked_for, 0, local_count - 1), axis=1)
    return chosen * (asked_for >= 0).astype(jnp.float32)[None, :, None, None]


def shards(
    rho_low,
    kprev_low,
    rho_band,
    kprev_band,
    hamiltonian,
    state_site,
    coupling_mag,
    coupling_phase,
    damping_rate,
    low_mode,
    occupation,
    couple_src,
    couple_mode,
    couple_dir,
):
    band_size = lax.axis_size("band")
    own_index = lax.axis_index("band")
    low_count = rho_low.shape[1]
    local_count = rho_band.shape[1]
    y_low = rho_low + section_weight * kprev_low
    y_band = rho_band + section_weight * kprev_band
    site_mask = site_masks(state_site, coupling_mag.shape[0])
    shifted = couple_src - low_count
    owner_dev = jnp.where(couple_src >= low_count, shifted // local_count, own_index)
    remote = owner_dev != own_index
    slot_index = shifted % local_count
    wanted = jnp.full((band_size + 1,), -1, jnp.int32)
    wanted = wanted.at[jnp.where(remote, owner_dev, band_size).ravel()].max(
        jnp.where(remote, slot_index, -1).ravel()
    )
    wanted = wanted[:band_size]
    asked_for = lax.all_to_all(wanted, "band", split_axis=0, concat_axis=0, tiled=True)
    gathered = lax.all_to_all(
        select_ados(y_band, asked_for), "band", split_axis=1, concat_axis=1, tiled=True
    )
    source_pool = jnp.concatenate([y_low, y_band, gathered], axis=1)
    position = jnp.where(
        couple_src < low_count,
        jnp.maximum(couple_src, 0),
        jnp.where(
            remote,
            low_count + local_count + owner_dev,
            low_count + shifted - own_index * local_count,
        ),
    )
    start_partial = jnp.zeros(y_low.shape, jnp.float32)
    k_band, low_partial = band_block(
        y_band,
        position,
        couple_src,
        couple_mode,
        couple_dir,
        occupation,
        source_pool,
        hamiltonian,
        site_mask,
        coupling_mag,
        coupling_phase,
        damping_rate,
        low_mode,
        start_partial,
    )
    rest_terms = low_rest(y_low, site_mask, coupling_mag, coupling_phase, damping_rate, low_mode)
    summed = lax.psum(low_partial, "band")
    k_low = commutator(hamiltonian, y_low) + rest_terms + summed
    return (k_low, k_band)


def solution(mesh):
    placed = (
        P(),
        P(),
        P(None, "band", None, None),
        P(None, "band", None, None),
        P(),
        P(),
        P(),
        P(),
        P(),
        P(),
        P("band", None),
        P("band", None),
        P("band", None),
        P("band", None),
    )
    return jax.shard_map(
        shards,
        mesh=mesh,
        in_specs=placed,
        out_specs=(P(), P(None, "band", None, None)),
        check_vma=False,
    )
```

profile of v0, /device:TPU:0, one launch (start us, length us, event | category | flops | bytes accessed | tf_op | source)
XLA Modules:
  0.0 624.7 jit_solution(5183368611853400584)
XLA Ops:
  11.3 7.3 %all-to-all-start = ((s32[32,1,1]{2,1,0:T(1,128)}), s32[32,1,1]{2,1,0:T(1,128)S(1)}, u32[]{:S(2)}, u32[]{:S(2)}) async-start(s32[32,1,1]{2,1,0:T(1,128)} %copy.168), calls=%async_computation | async-start | bytes 32768 | tf_op jit(solution)/shard_map/all_to_all | solution.py:155
  33.3 5.1 multiply_bitcast_fusion
  38.4 5.6 copy.170
  44.1 6.0 all-to-all-start.1
  63.8 5.6 copy.142
  69.5 5.7 copy.141
  92.5 51.2 %all-to-all-done.1 = f32[2,32,128,128]{2,3,0,1:T(8,128)} async-done(((f32[2,32,128,128]{2,3,0,1:T(8,128)}), f32[2,32,128,128]{2,3,0,1:T(8,128)}, u32[]{:S(2)}, u32[]{:S(2)}) %all-to-all-start.1) | async-done | bytes 4194336 | tf_op jit(solution)/shard_map/all_to_all | solution.py:156
  143.7 8.9 %pad_maximum_fusion = f32[2,80,128,128]{2,3,1,0:T(8,128)} fusion(f32[2,16,128,128]{2,3,1,0:T(8,128)S(1)} %multiply_add_fusion.1, f32[2,32,128,128]{2,3,1,0:T(8,128)} %copy-done.4, f32[2,32,128,128]{2,3,0,1:T(8,128)} %all-to-all-done.1), kind=kLoop, calls=%fused_computation.66 | loop fusion | flops 5242880 | bytes 20971520 | tf_op jit(solution)/shard_map/concatenate | solution.py:159
  152.6 11.4 %copy.176 = f32[2,80,128,128]{3,2,1,0:T(8,128)} copy(f32[2,80,128,128]{2,3,1,0:T(8,128)} %pad_maximum_fusion) | data formatting | bytes 20971520
  166.6 289.4 %while.16 = (s32[]{:T(128)}, f32[2,16,128,128]{3,2,1,0:T(8,128)}, f32[2,32,128,128]{3,2,1,0:T(8,128)}, s32[16,16]{0,1:T(8,128)S(1)}, s32[16,16]{0,1:T(8,128)S(1)...) while((s32[]{:T(128)}, f32[2,16,128,128]{3,2,1,0:T(8,128)}, ...), condition=%wide.region_4.5_spmd.clone, body=%wide.region_2.4_spmd.clone.sunk | while | flops 7886498 | bytes 54613344 | solution.py:114
  170.0 4.7 gather_fusion.5
  179.9 5.0 scatter_fusion
  198.2 5.0 scatter_fusion
  216.6 5.0 scatter_fusion
  234.9 5.0 scatter_fusion
  253.3 5.0 scatter_fusion
  271.6 5.0 scatter_fusion
  290.0 5.0 scatter_fusion
  308.3 5.0 scatter_fusion
  433.4 4.7 scatter_fusion
  456.0 5.9 copy.178
  476.8 127.2 %all-reduce.2.cloned.1.call-done = f32[2,32,128,128]{2,3,1,0:T(8,128)} async-done(((f32[2,32,128,128]{2,3,1,0:T(8,128)}), f32[2,32,128,128]{2,3,1,0:T(8,128)}) %all-reduce.2.cloned.1.call-update) | async-done | bytes 4194320 | tf_op jit(solution)/shard_map/psum | solution.py:187
  604.1 7.7 %fusion.23 = f32[2,32,128,128]{2,3,1,0:T(8,128)} fusion(f32[2,32,128,128]{2,3,1,0:T(8,128)} %all-reduce.2.cloned.1.call-done, f32[1,32,128,128]{2,3,1,0:T(8,128)S(1)} %fusion.34, f32[1,32,128,128]{2,3,1,0:T(8,128)} %fusion.36, f32[1,31,128,128]{2,3,1,0:T(8,128)} %get-tuple-element.446, f32[1,31,128,128]{2,3,1,0:T(8,128)} %get-tuple-element.447, ...), kind=kLoop, calls=%fused_computation.68 | loop fusion | flops 7340032 | bytes 20971648 | tf_op jit(solution)/shard_map/add | solution.py:188
  611.8 5.6 copy.179
  (497 shorter events, 305.2 us)
Async XLA Ops:
  7.2 43.1 %copy-start = (f32[72]{0:T(128)S(1)}, f32[72]{0:T(128)}, u32[]{:S(2)}) copy-start(f32[72]{0:T(128)} %param.24) | copy-start | bytes 868
  11.3 16.6 %all-to-all-start = ((s32[32,1,1]{2,1,0:T(1,128)}), s32[32,1,1]{2,1,0:T(1,128)S(1)}, u32[]{:S(2)}, u32[]{:S(2)}) async-start(s32[32,1,1]{2,1,0:T(1,128)} %copy.168), calls=%async_computation | async-start | bytes 32768 | tf_op jit(solution)/shard_map/all_to_all | solution.py:155
  18.6 3.0 copy-start.11
  44.1 6.2 copy-start.12
  44.1 6.4 %copy-start.8 = (f32[2,128,128]{2,1,0:T(8,128)S(1)}, f32[2,128,128]{2,1,0:T(8,128)}, u32[]{:S(2)}) copy-start(f32[2,128,128]{2,1,0:T(8,128)} %param.20) | copy-start | bytes 393220
  44.1 99.7 %all-to-all-start.1 = ((f32[2,32,128,128]{2,3,0,1:T(8,128)}), f32[2,32,128,128]{2,3,0,1:T(8,128)}, u32[]{:S(2)}, u32[]{:S(2)}) async-start(f32[2,32,128,128]{2,3,0,1:T(8,128)} %copy.170), calls=%async_computation.1 | async-start | bytes 8388608 | tf_op jit(solution)/shard_map/all_to_all | solution.py:156
  50.0 554.0 %all-reduce.2.cloned.1.call-start = ((), (), s32[]{:S(2)}) async-start(), calls=%async_computation.2 | async-start | bytes 8388608 | tf_op jit(solution)/shard_map/psum | solution.py:187
  60.6 3.1 copy-start.14
  60.6 3.1 copy-start.15
  69.4 5.7 copy-start.16
  69.4 6.4 %copy-start.13 = (s32[128]{0:T(128)S(1)}, s32[128]{0:T(128)}, u32[]{:S(2)}) copy-start(s32[128]{0:T(128)} %param.21) | copy-start | bytes 1540
  69.5 7.1 %copy-start.3 = (f32[72]{0:T(128)S(1)}, f32[72]{0:T(128)}, u32[]{:S(2)}) copy-start(f32[72]{0:T(128)} %param.23) | copy-start | bytes 868
  69.5 7.8 %copy-start.2 = (f32[72]{0:T(128)S(1)}, f32[72]{0:T(128)}, u32[]{:S(2)}) copy-start(f32[72]{0:T(128)} %param.22) | copy-start | bytes 868
  82.3 6.9 %copy-start.4 = (f32[2,32,128,128]{2,3,1,0:T(8,128)}, f32[2,32,128,128]{2,3,1,0:T(8,128)S(1)}, u32[]{:S(2)}) copy-start(f32[2,32,128,128]{2,3,1,0:T(8,128)S(1)} %multiply_add_fusion) | copy-start | bytes 12582916
  174.7 1.6 copy-start.6
  193.0 1.6 copy-start.6
  266.4 1.6 copy-start.6
  284.8 1.6 copy-start.6
  357.1 1.6 copy-start.6
  410.2 1.6 copy-start.6
  461.9 3.6 copy-start.5
  469.5 1.8 copy-start.9
  469.5 2.2 copy-start.10
  611.8 5.6 copy-start.1
  (26 other events, 41.4 us)
Sparse Core Ops, SparseCore 0:
  462.0 141.9 all-reduce.1
where the time goes:
time: 632 us; the launch traced here: 625 us
  local copies, waits for them, and re-layouts  242 us (38%)
  waiting for transfers between devices  178 us (28%)
  other arithmetic  144 us (23%)
  matrix products  29.6 us (5%)
  between operations  14.8 us (2%)
  starting transfers between devices  13.5 us (2%)
    psum x1, waiting for transfers between devices, shards(): summed = lax.psum(low_partial, 'band')  127 us
    scatter-add x16, other arithmetic, column(): low_partial = low_partial.at[:, target].add(back_term)  76.4 us
    gather x16, local copies, waits for them, and re-layouts, column(): fetched = jnp.take(source_pool, position[:, col_id], axis=1)  74.6 us
    while x96, local copies, waits for them, and re-layouts  54.7 us
    all_to_all x1, waiting for transfers between devices, shards(): lax.all_to_all(select_ados(y_band, asked_for), 'band', split_axis=1, conc...  51.2 us
    unnamed x40, local copies, waits for them, and re-layouts  37.6 us
    add x17, other arithmetic, couple_term(): x_imag = real_part * source[1] + imag_part * source[0]  18.3 us
    dot_general x8, matrix products, right_mul(): return jnp.einsum('jac,cb->jab', block, matrix, precision=highest)  15 us
  transfers between devices with their start and end apart: 3, of which 2 were waited for; matrix products, arithmetic and copies ran while one was open for 11% of the time, Pallas kernels for 0%

commit v1 on v0

v1 whole, which is shorter than its diff:
```python
import functools

import jax
import jax.numpy as jnp
from jax import lax
from jax.experimental import pallas as pl
from jax.experimental.pallas import tpu as pltpu
from jax.sharding import PartitionSpec as P

EXPS = 3
section_weight = 0.2
highest = lax.Precision.HIGHEST
VMEM_LIMIT = 60 * 1024 * 1024

vmem = pl.BlockSpec(memory_space=pltpu.VMEM)
smem = pl.BlockSpec(memory_space=pltpu.SMEM)
hbm = pl.BlockSpec(memory_space=pl.ANY)


def fill_masks(col_ref, row_ref, diff_ref, sum_ref):
    sites, size = diff_ref.shape[0], diff_ref.shape[1]

    def one_site(s, carry):
        va = jnp.where(col_ref[...] == s, 1.0, 0.0)
        vb = jnp.where(row_ref[...] == s, 1.0, 0.0)
        va = jnp.broadcast_to(va, (size, size))
        vb = jnp.broadcast_to(vb, (size, size))
        diff_ref[s] = va - vb
        if sum_ref is not None:
            sum_ref[s] = va + vb
        return carry

    lax.fori_loop(0, sites, one_site, 0)


def commutator(left, right, y_pair):
    size = y_pair.shape[-1]
    lhs = jnp.dot(
        left,
        y_pair.reshape(2 * size, size),
        precision=highest,
        preferred_element_type=jnp.float32,
    )
    rhs = jnp.dot(
        jnp.concatenate([y_pair[0], y_pair[1]], axis=1),
        right,
        precision=highest,
        preferred_element_type=jnp.float32,
    )
    return lhs[:size] - rhs[:, :size], lhs[size:] - rhs[:, size:]


def send_kernel(asked, rho, kprev, y_out, send, sems):
    count = rho.shape[1]
    peers = send.shape[0]

    def advance(i, carry):
        for part in range(2):
            y_out[i, part] = rho[part, i] + section_weight * kprev[part, i]
        return carry

    lax.fori_loop(0, count, advance, 0)

    def start(i, carry):
        pltpu.make_async_copy(y_out.at[asked[i]], send.at[i], sems.at[i]).start()
        return carry

    def finish(i, carry):
        pltpu.make_async_copy(y_out.at[0], send.at[i], sems.at[i]).wait()
        return carry

    lax.fori_loop(0, peers, start, 0)
    lax.fori_loop(0, peers, finish, 0)


def low_kernel(
    own_op,
    own_int,
    own_flt,
    count,
    target,
    site,
    alpha,
    y_band,
    rho_own,
    kprev_own,
    rho_top,
    kprev_top,
    left,
    right,
    col,
    row,
    out,
    diff,
    summ,
):
    size = out.shape[-1]
    step = pl.program_id(0)
    half = size // 2

    @pl.when(step == 0)
    def _():
        fill_masks(col, row, diff, summ)

        def clear(j, carry):
            out[0, j] = jnp.zeros((size, size), jnp.float32)
            out[1, j] = jnp.zeros((size, size), jnp.float32)
            return carry

        lax.fori_loop(0, out.shape[1], clear, 0)

        def operator(n, carry):
            def term(c, inner):
                j, s, amp = target[n, c], site[n, c], alpha[n, c]
                for part in range(2):
                    rows = pl.ds(part * half, half)
                    weight = amp * diff[s, rows]
                    out[0, j, rows] += weight * y_band[n, 1, rows]
                    out[1, j, rows] -= weight * y_band[n, 0, rows]
                return inner

            return lax.fori_loop(0, count[n], term, carry)

        lax.fori_loop(0, y_band.shape[0], operator, 0)

    @pl.when(own_int[step, 0] == 1)
    def _():
        j, s = own_op[step], own_int[step, 1]
        damping, amp, amp_cos, amp_sin = (own_flt[step, i] for i in range(4))
        own = rho_own[:, 0] + section_weight * kprev_own[:, 0]
        real, imag = commutator(left[...], right[...], own)
        top = rho_top[:, 0] + section_weight * kprev_top[:, 0]
        w_re, w_im = amp_cos * diff[s], amp_sin * summ[s]
        out[0, j] += imag - damping * own[0] + (w_re * top[1] + w_im * top[0])
        out[1, j] += -real - damping * own[1] + (w_im * top[1] - w_re * top[0])
        up = amp * diff[s]
        out[0, 0] += up * own[1]
        out[1, 0] -= up * own[0]


def add_terms(n, rows, count, source, site, alpha, beta, fetch, diff, summ, start):
    def term(c, state):
        re, im = state
        m, s = source[n, c], site[n, c]
        w_re = alpha[n, c] * diff[s, rows]
        w_im = beta[n, c] * summ[s, rows]
        y_re, y_im = fetch(m, rows)
        return re + (w_re * y_im + w_im * y_re), im + (w_im * y_im - w_re * y_re)

    return lax.fori_loop(0, count[n], term, start)


def local_kernel(
    count,
    source,
    site,
    alpha,
    beta,
    damping,
    y_band,
    rho_low,
    kprev_low,
    left,
    right,
    col,
    row,
    out,
    pool,
    diff,
    summ,
):
    size = out.shape[-1]
    low_count, band_count = rho_low.shape[1], y_band.shape[0]
    half = size // 2
    fill_masks(col, row, diff, summ)

    def advance(i, carry):
        for part in range(2):
            pool[i, part] = rho_low[part, i] + section_weight * kprev_low[part, i]
        return carry

    lax.fori_loop(0, low_count, advance, 0)

    def keep(i, carry):
        pool[low_count + i] = y_band[i]
        return carry

    lax.fori_loop(0, band_count, keep, 0)

    def operator(n, carry):
        y_pair = y_band[n]
        real, imag = commutator(left[...], right[...], y_pair)
        out[0, n] = imag - damping[n] * y_pair[0]
        out[1, n] = -real - damping[n] * y_pair[1]
        for part in range(2):
            rows = pl.ds(part * half, half)
            re, im = add_terms(
                n,
                rows,
                count,
                source,
                site,
                alpha,
                beta,
                lambda m, r: (pool[m, 0, r], pool[m, 1, r]),
                diff,
                summ,
                (out[0, n, rows], out[1, n, rows]),
            )
            out[0, n, rows] = re
            out[1, n, rows] = im
        return carry

    lax.fori_loop(0, band_count, operator, 0)


def far_kernel(
    count, source, site, alpha, beta, received, base, col, row, out, diff, summ
):
    sites, block, size = diff.shape
    step = pl.program_id(0)

    def one_site(s, carry):
        va = jnp.where(col[...] == s, 1.0, 0.0)
        vb = jnp.where(row[...] == s, 1.0, 0.0)
        va = jnp.broadcast_to(va, (block, size))
        vb = jnp.broadcast_to(vb, (block, size))
        diff[s] = va - vb
        summ[s] = va + vb
        return carry

    lax.fori_loop(0, sites, one_site, 0)
    rows = pl.ds(0, block)

    def operator(n, carry):
        re, im = add_terms(
            n,
            rows,
            count,
            source,
            site,
            alpha,
            beta,
            lambda m, r: (received[m, 0, r], received[m, 1, r]),
            diff,
            summ,
            (base[0, n], base[1, n]),
        )
        out[0, n] = re
        out[1, n] = im
        return carry

    lax.fori_loop(0, out.shape[1], operator, 0)


def compact(flag, arrays):
    width = flag.shape[1]
    place = jnp.cumsum(flag.astype(jnp.int32), axis=1) - 1
    hit = (place[:, :, None] == jnp.arange(width)[None, None, :]) & flag[:, :, None]
    packed = [jnp.sum(jnp.where(hit, a[:, :, None], 0), axis=1).astype(a.dtype) for a in arrays]
    return jnp.sum(flag.astype(jnp.int32), axis=1), packed


def pick(index, table):
    hit = index[..., None] == jnp.arange(table.shape[-1], dtype=index.dtype)
    return jnp.sum(jnp.where(hit, table, 0), axis=-1).astype(table.dtype)


def shards(
    rho_low,
    kprev_low,
    rho_band,
    kprev_band,
    hamiltonian,
    state_site,
    coupling_mag,
    coupling_phase,
    damping_rate,
    low_mode,
    occupation,
    couple_src,
    couple_mode,
    couple_dir,
):
    band_size = lax.axis_size("band")
    own_index = lax.axis_index("band")
    low_count = rho_low.shape[1]
    band_count = rho_band.shape[1]
    size = rho_band.shape[-1]
    modes = coupling_mag.shape[0]
    sites = modes // EXPS
    f32 = jnp.float32
    params = functools.partial(pltpu.CompilerParams, vmem_limit_bytes=VMEM_LIMIT)

    shifted = couple_src - low_count
    owner = jnp.where(couple_src >= low_count, shifted // band_count, own_index)
    remote = owner != own_index
    slot = shifted % band_count
    asks = remote[None] & (owner[None] == jnp.arange(band_size)[:, None, None])
    wanted = jnp.max(jnp.where(asks, slot[None], 0), axis=(1, 2))
    asked = lax.all_to_all(wanted, "band", split_axis=0, concat_axis=0, tiled=True)

    y_band, send = pl.pallas_call(
        send_kernel,
        in_specs=[smem, vmem, vmem],
        out_specs=[vmem, hbm],
        out_shape=[
            jax.ShapeDtypeStruct((band_count, 2, size, size), f32),
            jax.ShapeDtypeStruct((band_size, 2, size, size), f32),
        ],
        scratch_shapes=[pltpu.SemaphoreType.DMA((band_size,))],
        compiler_params=params(),
        name="send",
    )(asked, rho_band, kprev_band)
    received = lax.all_to_all(send, "band", split_axis=0, concat_axis=0, tiled=True)

    level = jnp.sum(
        jnp.where(
            couple_mode[:, :, None] == jnp.arange(modes)[None, None, :],
            occupation[:, None, :],
            0,
        ),
        axis=-1,
    ).astype(f32)
    strength = pick(couple_mode, coupling_mag)
    cos_mode, sin_mode = jnp.cos(coupling_phase), jnp.sin(coupling_phase)
    is_down = couple_dir == 1
    amp_down = jnp.sqrt(level * strength)
    alpha = jnp.where(
        is_down, amp_down * pick(couple_mode, cos_mode), jnp.sqrt((level + 1.0) * strength)
    )
    beta = jnp.where(is_down, amp_down * pick(couple_mode, sin_mode), 0.0)
    site = couple_mode // EXPS
    live = couple_src >= 0
    is_low = live & (couple_src < low_count)
    position = jnp.where(couple_src < low_count, couple_src, low_count + slot)
    marks = jnp.concatenate([jnp.full((1,), -1, jnp.int32), low_mode])
    held = (pick(jnp.clip(couple_src, 0, low_count - 1), marks) == couple_mode).astype(f32)
    alpha_low = jnp.sqrt((held + 1.0) * strength)
    damping = jnp.dot(occupation.astype(f32), damping_rate, precision=highest)
    low_n, (low_j, low_s, low_a) = compact(is_low, [couple_src, site, alpha_low])
    near_n, near = compact(live & ~remote, [position, site, alpha, beta])
    far_n, far = compact(live & remote, [owner, site, alpha, beta])

    h_re, h_im = hamiltonian[0], hamiltonian[1]
    left = jnp.block([[h_re, -h_im], [h_im, h_re]])
    right = jnp.block([[h_re, h_im], [-h_im, h_re]])
    col, row = state_site[:, None], state_site[None, :]

    turns = -(-low_count // band_size)
    own_op = own_index + band_size * jnp.arange(turns, dtype=jnp.int32)
    own_here = own_op < low_count
    own_op = jnp.minimum(own_op, low_count - 1)
    own_mode = pick(jnp.maximum(own_op - 1, 0), low_mode)
    raised = (own_op >= 1).astype(f32)
    own_amp = jnp.sqrt(pick(own_mode, coupling_mag)) * raised
    own_int = jnp.stack([own_here.astype(jnp.int32), own_mode // EXPS], axis=1)
    own_flt = jnp.stack(
        [
            pick(own_mode, damping_rate) * raised,
            own_amp,
            own_amp * pick(own_mode, cos_mode),
            own_amp * pick(own_mode, sin_mode),
        ],
        axis=1,
    )
    own_block = pl.BlockSpec((2, 1, size, size), lambda g, ops: (0, ops[g], 0, 0))
    top_block = pl.BlockSpec((2, 1, size, size), lambda g, ops: (0, 0, 0, 0))
    partial = pl.pallas_call(
        low_kernel,
        grid_spec=pltpu.PrefetchScalarGridSpec(
            num_scalar_prefetch=1,
            grid=(turns,),
            in_specs=[smem] * 6
            + [vmem, own_block, own_block, top_block, top_block]
            + [vmem] * 4,
            out_specs=vmem,
            scratch_shapes=[pltpu.VMEM((sites, size, size), f32)] * 2,
        ),
        out_shape=jax.ShapeDtypeStruct((2, low_count, size, size), f32),
        compiler_params=params(),
        name="low",
    )(
        own_op,
        own_int,
        own_flt,
        low_n,
        low_j,
        low_s,
        low_a,
        y_band,
        rho_low,
        kprev_low,
        rho_low,
        kprev_low,
        left,
        right,
        col,
        row,
    )
    k_low = lax.psum(partial, "band")

    base = pl.pallas_call(
        local_kernel,
        in_specs=[smem] * 6 + [vmem] * 7,
        out_specs=vmem,
        out_shape=jax.ShapeDtypeStruct((2, band_count, size, size), f32),
        scratch_shapes=[pltpu.VMEM((low_count + band_count, 2, size, size), f32)]
        + [pltpu.VMEM((sites, size, size), f32)] * 2,
        compiler_params=params(),
        name="local",
    )(near_n, *near, damping, y_band, rho_low, kprev_low, left, right, col, row)

    block = size // 2
    k_band = pl.pallas_call(
        far_kernel,
        grid=(size // block,),
        in_specs=[smem] * 5
        + [
            pl.BlockSpec((band_size, 2, block, size), lambda g: (0, 0, g, 0)),
            pl.BlockSpec((2, band_count, block, size), lambda g: (0, 0, g, 0)),
            pl.BlockSpec((block, 1), lambda g: (g, 0)),
            pl.BlockSpec((1, size), lambda g: (0, 0)),
        ],
        out_specs=pl.BlockSpec((2, band_count, block, size), lambda g: (0, 0, g, 0)),
        out_shape=jax.ShapeDtypeStruct((2, band_count, size, size), f32),
        scratch_shapes=[pltpu.VMEM((sites, block, size), f32)] * 2,
        compiler_params=params(),
        name="far",
    )(far_n, *far, received, base, col, row)
    return (k_low, k_band)


def solution(mesh):
    placed = (
        P(),
        P(),
        P(None, "band", None, None),
        P(None, "band", None, None),
        P(),
        P(),
        P(),
        P(),
        P(),
        P(),
        P("band", None),
        P("band", None),
        P("band", None),
        P("band", None),
    )
    return jax.shard_map(
        shards,
        mesh=mesh,
        in_specs=placed,
        out_specs=(P(), P(None, "band", None, None)),
        check_vma=False,
    )
```

time: 632 us -> 256 us (0.41); the launches traced: 625 us -> 256 us
  local copies, waits for them, and re-layouts: 242 us -> 5.63 us
  other arithmetic: 144 us -> 14.3 us
  Pallas kernels: 0 us -> 47.5 us
  matrix products: 29.6 us -> 0.64 us
  waiting for transfers between devices: 178 us -> 150 us
  blocking collectives: 0 us -> 14.3 us
  starting transfers between devices: 13.5 us -> 3.76 us
    gather x101 -> x0, local copies, waits for them, and re-layouts: 133 us -> none  [the longest x16 74.6 us: column(): fetched = jnp.take(source_pool, position[:, col_id], axis=1)]
    scatter-add x16 -> x0, other arithmetic: 76.4 us -> none  [column(): low_partial = low_partial.at[:, target].add(back_term)]
    while x97 -> x0, local copies, waits for them, and re-layouts: 60.6 us -> none
    pallas_call x0 -> x4, Pallas kernels: none -> 47.5 us  [the longest x1 21.2 us: shards(): pl.pallas_call(local_kernel, in_specs=[smem] * 6 + [vmem] * 7, out_specs=...]
    psum x1, waiting for transfers between devices: 127 us -> 80.3 us  [shards(): k_low = lax.psum(partial, 'band')]
    add x36 -> x0, other arithmetic: 39 us -> none  [the longest x17 18.3 us: couple_term(): x_imag = real_part * source[1] + imag_part * source[0]]
    unnamed x40 -> x21, local copies, waits for them, and re-layouts: 37.6 us -> 4.76 us
    dot_general x17 -> x1, matrix products: 29.6 us -> 0.64 us  [shards(): damping = jnp.dot(occupation.astype(f32), damping_rate, precision=highest)]
  transfers between devices with their start and end apart: 3 -> 2, of which waited for: 2 -> 2; matrix products, arithmetic and copies ran while one was open for 11% -> 5% of each run, Pallas kernels for 0% -> 16%
where the time goes in v1:
time: 256 us
  waiting for transfers between devices  150 us (59%)
  Pallas kernels  47.5 us (19%)
  between operations  19 us (7%)
  other arithmetic  14.3 us (6%)
  blocking collectives  14.3 us (6%)
  local copies, waits for them, and re-layouts  5.63 us (2%)
  starting transfers between devices  3.76 us (1%)
    psum x1, waiting for transfers between devices, shards(): k_low = lax.psum(partial, 'band')  80.3 us
    all_to_all x1, waiting for transfers between devices, shards(): lax.all_to_all(send, 'band', split_axis=0, concat_axis=0, tiled=True)  70 us
    pallas_call x1, Pallas kernels, shards(): pl.pallas_call(local_kernel, in_specs=[smem] * 6 + [vmem] * 7, out_specs=...  21.2 us
    all_to_all x1, blocking collectives, shards(): lax.all_to_all(wanted, 'band', split_axis=0, concat_axis=0, tiled=True)  14.3 us
    pallas_call x1, Pallas kernels, shards(): pl.pallas_call(far_kernel, grid=(size // block,), in_specs=[smem] * 5 + [...  12.4 us
    pallas_call x1, Pallas kernels, shards(): pl.pallas_call(low_kernel, grid_spec=pltpu.PrefetchScalarGridSpec(num_sca...  7.82 us
    pallas_call x1, Pallas kernels, shards(): pl.pallas_call(send_kernel, in_specs=[smem, vmem, vmem], out_specs=[vmem,...  6.13 us
  transfers between devices with their start and end apart: 2, of which 2 were waited for; matrix products, arithmetic and copies ran while one was open for 5% of the time, Pallas kernels for 16%

profile of v1, /device:TPU:0, one launch (start us, length us, event | category | flops | bytes accessed | tf_op | source)
XLA Modules:
  0.0 255.6 jit_solution(10602136105611492708)
XLA Ops:
  7.2 1.4 convert_reduce_fusion
  8.8 14.3 %all_to_all.16 = s32[32,1,1]{2,1,0:T(1,128)S(1)} all-to-all(s32[32,1,1]{2,1,0:T(1,128)S(1)} %copy.27), channel_id=1, replica_groups=mesh['band'=32] {'band'}, dimensions={0} | all-to-all | bytes 256 | tf_op jit(solution)/shard_map/all_to_all | solution.py:301
  23.1 1.3 reduce.10.asked
  24.4 6.1 %send.1 = (f32[16,2,128,128]{3,2,1,0:T(8,128)}, f32[32,2,128,128]{3,2,1,0:T(8,128)}) custom-call(s32[32]{0:T(128)} %reduce.10.asked, f32[2,16,128,128]{3,2,1,0:T(8,128)} %rho.1, f32[2,16,128,128]{3,2,1,0:T(8,128)} %kprev.1), custom_call_target="tpu_custom_call" | custom-call | tf_op jit(solution)/shard_map/send/pallas_call | solution.py:303
  30.7 3.7 %all-to-all-start.1 = ((f32[32,2,128,128]{3,2,1,0:T(8,128)}), f32[32,2,128,128]{3,2,1,0:T(8,128)}, u32[]{:S(2)}, u32[]{:S(2)}) async-start(f32[32,2,128,128]{3,2,1,0:T(8,128)} %get-tuple-element.5), calls=%async_computation.1 | async-start | bytes 8388608 | tf_op jit(solution)/shard_map/all_to_all | solution.py:315
  34.4 0.7 fusion.11
  37.2 1.4 select_reduce_fusion.19
  40.0 1.4 select_reduce_fusion.17
  43.1 0.7 convert_reduce_fusion.1
  43.9 0.7 copy.28.col
  44.7 0.6 pad_add_fusion.own_int
  45.4 0.6 pad_maximum_fusion.4.own_flt
  46.0 0.7 convert_reduce_fusion.2.count
  47.9 0.8 select_reduce_fusion.12.alpha
  48.7 0.9 fusion.1
  49.6 1.2 select_reduce_fusion.2
  50.7 7.8 %low.1 = f32[2,32,128,128]{3,2,1,0:T(8,128)} custom-call(s32[1]{0:T(128)} %bitcast.own_op, s32[1,2]{1,0:T(1,128)} %pad_add_fusion.own_int, f32[1,4]{1,0:T(1,128)} %pad_maximum_fusion.4.own_flt, s32[16]{0:T(128)} %convert_reduce_fusion.2.count, s32[16,16]{1,0:T(8,128)} %get-tuple-element.20.target, s32[16,16]{1,0:T(8,128)} %get-tuple-element.21.site, ...), custom_call_target="tpu_custom_call" | custom-call | tf_op jit(solution)/shard_map/low/pallas_call | solution.py:369
  58.6 0.6 convolution_bitcast_fusion.damping
  59.2 0.9 select_reduce_fusion.4
  60.1 21.2 %local.1.base = f32[2,16,128,128]{3,2,1,0:T(8,128)} custom-call(s32[16]{0:T(128)} %get-tuple-element.25.count, s32[16,16]{1,0:T(8,128)} %get-tuple-element.9.source, s32[16,16]{1,0:T(8,128)} %get-tuple-element.8.site, f32[16,16]{1,0:T(8,128)} %get-tuple-element.12.alpha, f32[16,16]{1,0:T(8,128)} %get-tuple-element.13.beta, ...), custom_call_target="tpu_custom_call" | custom-call | tf_op jit(solution)/shard_map/local/pallas_call | solution.py:403
  81.3 70.0 %all-to-all-done.1.received = f32[32,2,128,128]{3,2,1,0:T(8,128)} async-done(((f32[32,2,128,128]{3,2,1,0:T(8,128)}), f32[32,2,128,128]{3,2,1,0:T(8,128)}, u32[]{:S(2)}, u32[]{:S(2)}) %all-to-all-start.1) | async-done | bytes 4194336 | tf_op jit(solution)/shard_map/all_to_all | solution.py:315
  151.3 12.4 %far.1 = f32[2,16,128,128]{3,2,1,0:T(8,128)} custom-call(s32[16]{0:T(128)} %get-tuple-element.31.count, s32[16,16]{1,0:T(8,128)} %get-tuple-element.18.source, s32[16,16]{1,0:T(8,128)} %get-tuple-element.19.site, f32[16,16]{1,0:T(8,128)} %get-tuple-element.11.alpha, f32[16,16]{1,0:T(8,128)} %get-tuple-element.10.beta, ...), custom_call_target="tpu_custom_call" | custom-call | tf_op jit(solution)/shard_map/far/pallas_call | solution.py:415
  163.8 80.3 %all-reduce.2.cloned.1.call-done = f32[2,32,128,128]{3,2,1,0:T(8,128)} async-done(((f32[2,32,128,128]{3,2,1,0:T(8,128)}), f32[2,32,128,128]{3,2,1,0:T(8,128)}) %all-reduce.2.cloned.1.call-update) | async-done | bytes 4194320 | tf_op jit(solution)/shard_map/psum | solution.py:401
  244.0 4.7 %copy.32 = f32[2,32,128,128]{3,2,1,0:T(8,128)} copy(f32[2,32,128,128]{3,2,1,0:T(8,128)} %all-reduce.2.cloned.1.call-done) | data formatting | bytes 8388608
  (42 shorter events, 2.2 us)
Async XLA Ops:
  30.5 3.9 %copy-start.9 = (s32[31]{0:T(128)S(1)}, s32[31]{0:T(128)}, u32[]{:S(2)}) copy-start(s32[31]{0:T(128)} %param.23) | copy-start | bytes 376
  30.5 6.6 %copy-start.6 = (f32[72]{0:T(128)S(1)}, f32[72]{0:T(128)}, u32[]{:S(2)}) copy-start(f32[72]{0:T(128)} %param.20) | copy-start | bytes 868
  30.6 6.6 %copy-start.7 = (f32[72]{0:T(128)S(1)}, f32[72]{0:T(128)}, u32[]{:S(2)}) copy-start(f32[72]{0:T(128)} %param.22) | copy-start | bytes 868
  30.6 9.4 %copy-start.8 = (f32[72]{0:T(128)S(1)}, f32[72]{0:T(128)}, u32[]{:S(2)}) copy-start(f32[72]{0:T(128)} %param.21) | copy-start | bytes 868
  30.6 12.1 %copy-start.1 = (s32[16,16]{1,0:T(8,128)S(1)}, s32[16,16]{1,0:T(8,128)}, u32[]{:S(2)}) copy-start(s32[16,16]{1,0:T(8,128)} %param.25) | copy-start | bytes 3076
  30.6 13.3 %copy-start.4 = (s32[128]{0:T(128)S(1)}, s32[128]{0:T(128)}, u32[]{:S(2)}) copy-start(s32[128]{0:T(128)} %param.19) | copy-start | bytes 1540
  30.6 16.5 %copy-start.2 = (s32[16,16]{1,0:T(8,128)S(1)}, s32[16,16]{1,0:T(8,128)}, u32[]{:S(2)}) copy-start(s32[16,16]{1,0:T(8,128)} %param.26) | copy-start | bytes 3076
  30.6 16.5 %copy-start.3 = (s32[16,72]{1,0:T(8,128)S(1)}, s32[16,72]{1,0:T(8,128)}, u32[]{:S(2)}) copy-start(s32[16,72]{1,0:T(8,128)} %param.24) | copy-start | bytes 13828
  30.6 17.2 %copy-start.5 = (s32[16,16]{1,0:T(8,128)S(1)}, s32[16,16]{1,0:T(8,128)}, u32[]{:S(2)}) copy-start(s32[16,16]{1,0:T(8,128)} %param.27) | copy-start | bytes 3076
  30.6 18.0 %copy-start = (f32[2,128,128]{2,1,0:T(8,128)S(1)}, f32[2,128,128]{2,1,0:T(8,128)}, u32[]{:S(2)}) copy-start(f32[2,128,128]{2,1,0:T(8,128)} %param.18) | copy-start | bytes 393220
  30.7 120.7 %all-to-all-start.1 = ((f32[32,2,128,128]{3,2,1,0:T(8,128)}), f32[32,2,128,128]{3,2,1,0:T(8,128)}, u32[]{:S(2)}, u32[]{:S(2)}) async-start(f32[32,2,128,128]{3,2,1,0:T(8,128)} %get-tuple-element.5), calls=%async_computation.1 | async-start | bytes 8388608 | tf_op jit(solution)/shard_map/all_to_all | solution.py:315
  34.4 209.6 %all-reduce.2.cloned.1.call-start = ((), (), s32[]{:S(2)}) async-start(), calls=%async_computation.2 | async-start | bytes 8388608 | tf_op jit(solution)/shard_map/psum | solution.py:401
Sparse Core Ops, SparseCore 0:
  58.7 185.2 all-reduce.1

commit v2 on v1

--- a/solution.py
+++ b/solution.py
@@ -50,6 +50,99 @@
     return lhs[:size] - rhs[:, :size], lhs[size:] - rhs[:, size:]
 
 
+LOW_J, LOW_S, NEAR_M, NEAR_S, FAR_M, FAR_S, COUNTS, OWN_I = range(8)
+LOW_A, NEAR_A, NEAR_B, FAR_A, FAR_B, DAMP, OWN_F = range(7)
+
+
+def prep_kernel(
+    low_count, own, src, mode, direction, occ, mag, cos, sin, rate, low_mode, ints, flts
+):
+    rows, width = src.shape
+    modes = occ.shape[1]
+    others = low_mode.shape[1]
+    band_size = own[1]
+    own_index = own[0]
+    f32, i32 = jnp.float32, jnp.int32
+    lane_mode = lax.broadcasted_iota(i32, (rows, modes), 1)
+    lane_low = lax.broadcasted_iota(i32, (rows, others), 1)
+    lane_col = lax.broadcasted_iota(i32, (rows, width), 1)
+    occ_f = occ[...].astype(f32)
+    mag_b = jnp.broadcast_to(mag[...], (rows, modes))
+    cos_b = jnp.broadcast_to(cos[...], (rows, modes))
+    sin_b = jnp.broadcast_to(sin[...], (rows, modes))
+    rate_b = jnp.broadcast_to(rate[...], (rows, modes))
+    mark_b = jnp.broadcast_to(low_mode[...].astype(f32) + 1.0, (rows, others))
+
+    def total(x):
+        return jnp.sum(x, axis=1, keepdims=True)
+
+    zero_i = jnp.zeros((rows, width), i32)
+    zero_f = jnp.zeros((rows, width), f32)
+    int_out = [zero_i] * 6
+    flt_out = [zero_f] * 5
+    fill = [jnp.zeros((rows, 1), i32)] * 3
+    for c in range(width):
+        src_c, mode_c = src[:, c : c + 1], mode[:, c : c + 1]
+        down = direction[:, c : c + 1] == 1
+        hit = lane_mode == mode_c
+        level = total(jnp.where(hit, occ_f, 0.0))
+        strength = total(jnp.where(hit, mag_b, 0.0))
+        amp_down = jnp.sqrt(level * strength)
+        amp_up = jnp.sqrt((level + 1.0) * strength)
+        alpha = jnp.where(down, amp_down * total(jnp.where(hit, cos_b, 0.0)), amp_up)
+        beta = jnp.where(down, amp_down * total(jnp.where(hit, sin_b, 0.0)), 0.0)
+        mark = total(jnp.where(lane_low == src_c - 1, mark_b, 0.0))
+        held = jnp.where(mark == mode_c.astype(f32) + 1.0, 2.0, 1.0)
+        alpha_low = jnp.sqrt(held * strength)
+        site = mode_c // EXPS
+        live = src_c >= 0
+        is_low = live & (src_c < low_count)
+        shifted = jnp.maximum(src_c - low_count, 0)
+        owner = shifted // rows
+        local = is_low | (live & (owner == own_index))
+        near_m = jnp.where(is_low, src_c, low_count + shifted % rows)
+        lists = (
+            (is_low, (src_c, site), (alpha_low,)),
+            (local, (near_m, site), (alpha, beta)),
+            (live & ~local, (owner, site), (alpha, beta)),
+        )
+        at_f = 0
+        for which, (flag, int_cols, flt_cols) in enumerate(lists):
+            put = (lane_col == fill[which]) & flag
+            for i, value in enumerate(int_cols):
+                int_out[2 * which + i] = int_out[2 * which + i] + jnp.where(put, value, 0)
+            for value in flt_cols:
+                flt_out[at_f] = flt_out[at_f] + jnp.where(put, value, 0.0)
+                at_f += 1
+            fill[which] = fill[which] + jnp.where(flag, 1, 0)
+    for i in range(6):
+        ints[i] = int_out[i]
+    for i in range(5):
+        flts[i] = flt_out[i]
+    ints[COUNTS] = jnp.where(
+        lane_col == 0, fill[0], jnp.where(lane_col == 1, fill[1], fill[2])
+    )
+    flts[DAMP] = jnp.broadcast_to(total(occ_f * rate_b), (rows, width))
+    turn = lax.broadcasted_iota(i32, (rows, 1), 0)
+    op = own_index + band_size * turn
+    here = jnp.where(op < low_count, 1, 0)
+    op = jnp.minimum(op, low_count - 1)
+    op_mode = total(jnp.where(lane_low == jnp.maximum(op - 1, 0), mark_b, 0.0)) - 1.0
+    op_mode = op_mode.astype(i32)
+    hit = lane_mode == op_mode
+    raised = jnp.where(op >= 1, 1.0, 0.0)
+    amp = jnp.sqrt(total(jnp.where(hit, mag_b, 0.0))) * raised
+    amp_cos = amp * total(jnp.where(hit, cos_b, 0.0))
+    amp_sin = amp * total(jnp.where(hit, sin_b, 0.0))
+    damp = total(jnp.where(hit, rate_b, 0.0)) * raised
+    ints[OWN_I] = jnp.where(lane_col == 0, here, jnp.where(lane_col == 1, op_mode // EXPS, op))
+    flts[OWN_F] = jnp.where(
+        lane_col == 0,
+        damp,
+        jnp.where(lane_col == 1, amp, jnp.where(lane_col == 2, amp_cos, amp_sin)),
+    )
+
+
 def send_kernel(asked, rho, kprev, y_out, send, sems):
     count = rho.shape[1]
     peers = send.shape[0]
@@ -62,7 +155,7 @@
     lax.fori_loop(0, count, advance, 0)
 
     def start(i, carry):
-        pltpu.make_async_copy(y_out.at[asked[i]], send.at[i], sems.at[i]).start()
+        pltpu.make_async_copy(y_out.at[asked[i, 0, 0]], send.at[i], sems.at[i]).start()
         return carry
 
     def finish(i, carry):
@@ -74,13 +167,8 @@
 
 
 def low_kernel(
-    own_op,
-    own_int,
-    own_flt,
-    count,
-    target,
-    site,
-    alpha,
+    ints,
+    flts,
     y_band,
     rho_own,
     kprev_own,
@@ -111,7 +199,7 @@
 
         def operator(n, carry):
             def term(c, inner):
-                j, s, amp = target[n, c], site[n, c], alpha[n, c]
+                j, s, amp = ints[LOW_J, n, c], ints[LOW_S, n, c], flts[LOW_A, n, c]
                 for part in range(2):
                     rows = pl.ds(part * half, half)
                     weight = amp * diff[s, rows]
@@ -119,14 +207,14 @@
                     out[1, j, rows] -= weight * y_band[n, 0, rows]
                 return inner
 
-            return lax.fori_loop(0, count[n], term, carry)
+            return lax.fori_loop(0, ints[COUNTS, n, 0], term, carry)
 
         lax.fori_loop(0, y_band.shape[0], operator, 0)
 
-    @pl.when(own_int[step, 0] == 1)
+    @pl.when(ints[OWN_I, step, 0] == 1)
     def _():
-        j, s = own_op[step], own_int[step, 1]
-        damping, amp, amp_cos, amp_sin = (own_flt[step, i] for i in range(4))
+        s, j = ints[OWN_I, step, 1], ints[OWN_I, step, 2]
+        damping, amp, amp_cos, amp_sin = (flts[OWN_F, step, i] for i in range(4))
         own = rho_own[:, 0] + section_weight * kprev_own[:, 0]
         real, imag = commutator(left[...], right[...], own)
         top = rho_top[:, 0] + section_weight * kprev_top[:, 0]
@@ -138,25 +226,23 @@
         out[1, 0] -= up * own[0]
 
 
-def add_terms(n, rows, count, source, site, alpha, beta, fetch, diff, summ, start):
+def add_terms(n, rows, which, ints, flts, fetch, diff, summ, start):
+    count_at, source_at, alpha_at = which
+
     def term(c, state):
         re, im = state
-        m, s = source[n, c], site[n, c]
-        w_re = alpha[n, c] * diff[s, rows]
-        w_im = beta[n, c] * summ[s, rows]
+        m, s = ints[source_at, n, c], ints[source_at + 1, n, c]
+        w_re = flts[alpha_at, n, c] * diff[s, rows]
+        w_im = flts[alpha_at + 1, n, c] * summ[s, rows]
         y_re, y_im = fetch(m, rows)
         return re + (w_re * y_im + w_im * y_re), im + (w_im * y_im - w_re * y_re)
 
-    return lax.fori_loop(0, count[n], term, start)
+    return lax.fori_loop(0, ints[COUNTS, n, count_at], term, start)
 
 
 def local_kernel(
-    count,
-    source,
-    site,
-    alpha,
-    beta,
-    damping,
+    ints,
+    flts,
     y_band,
     rho_low,
     kprev_low,
@@ -189,19 +275,18 @@
 
     def operator(n, carry):
         y_pair = y_band[n]
+        damping = flts[DAMP, n, 0]
         real, imag = commutator(left[...], right[...], y_pair)
-        out[0, n] = imag - damping[n] * y_pair[0]
-        out[1, n] = -real - damping[n] * y_pair[1]
+        out[0, n] = imag - damping * y_pair[0]
+        out[1, n] = -real - damping * y_pair[1]
         for part in range(2):
             rows = pl.ds(part * half, half)
             re, im = add_terms(
                 n,
                 rows,
-                count,
-                source,
-                site,
-                alpha,
-                beta,
+                (1, NEAR_M, NEAR_A),
+                ints,
+                flts,
                 lambda m, r: (pool[m, 0, r], pool[m, 1, r]),
                 diff,
                 summ,
@@ -214,11 +299,8 @@
     lax.fori_loop(0, band_count, operator, 0)
 
 
-def far_kernel(
-    count, source, site, alpha, beta, received, base, col, row, out, diff, summ
-):
+def far_kernel(ints, flts, received, base, col, row, out, diff, summ):
     sites, block, size = diff.shape
-    step = pl.program_id(0)
 
     def one_site(s, carry):
         va = jnp.where(col[...] == s, 1.0, 0.0)
@@ -236,11 +318,9 @@
         re, im = add_terms(
             n,
             rows,
-            count,
-            source,
-            site,
-            alpha,
-            beta,
+            (2, FAR_M, FAR_A),
+            ints,
+            flts,
             lambda m, r: (received[m, 0, r], received[m, 1, r]),
             diff,
             summ,
@@ -253,17 +333,47 @@
     lax.fori_loop(0, out.shape[1], operator, 0)
 
 
-def compact(flag, arrays):
-    width = flag.shape[1]
-    place = jnp.cumsum(flag.astype(jnp.int32), axis=1) - 1
-    hit = (place[:, :, None] == jnp.arange(width)[None, None, :]) & flag[:, :, None]
-    packed = [jnp.sum(jnp.where(hit, a[:, :, None], 0), axis=1).astype(a.dtype) for a in arrays]
-    return jnp.sum(flag.astype(jnp.int32), axis=1), packed
-
-
-def pick(index, table):
-    hit = index[..., None] == jnp.arange(table.shape[-1], dtype=index.dtype)
-    return jnp.sum(jnp.where(hit, table, 0), axis=-1).astype(table.dtype)
+def sum_over_band(rows, band_size, own_index):
+    bits = band_size.bit_length() - 1
+    if 1 << bits != band_size or rows.shape[0] % (2 * band_size * 8):
+        return lax.psum(rows, "band")
+    plain = list(range(bits))
+    swapped = plain[:1] + plain[1:3][::-1] + plain[3:]
+    orders = (plain, swapped)
+    stream = rows.shape[0] // 2
+    starts = [jnp.int32(0), jnp.int32(stream)]
+    length = stream
+    flag = [(own_index >> b) & 1 for b in range(bits)]
+
+    def swap(x, bit):
+        pairs = [(i, i ^ (1 << bit)) for i in range(band_size)]
+        return lax.ppermute(x, "band", pairs)
+
+    for level in range(bits):
+        length //= 2
+        got, keep = [], []
+        for order, start in zip(orders, starts):
+            mine = flag[order[level]]
+            give = lax.dynamic_slice_in_dim(rows, start + (1 - mine) * length, length)
+            got.append(swap(give, order[level]))
+            keep.append(start + mine * length)
+        for other, start in zip(got, keep):
+            held = lax.dynamic_slice_in_dim(rows, start, length)
+            rows = lax.dynamic_update_slice_in_dim(rows, held + other, start, 0)
+        starts = keep
+    for level in reversed(range(bits)):
+        got = []
+        for order, start in zip(orders, starts):
+            got.append(swap(lax.dynamic_slice_in_dim(rows, start, length), order[level]))
+        moved = []
+        for order, start, other in zip(orders, starts, got):
+            mine = flag[order[level]]
+            base = start - mine * length
+            rows = lax.dynamic_update_slice_in_dim(rows, other, base + (1 - mine) * length, 0)
+            moved.append(base)
+        starts = moved
+        length *= 2
+    return rows
 
 
 def shards(
@@ -287,17 +397,16 @@
     low_count = rho_low.shape[1]
     band_count = rho_band.shape[1]
     size = rho_band.shape[-1]
-    modes = coupling_mag.shape[0]
-    sites = modes // EXPS
+    sites = coupling_mag.shape[0] // EXPS
     f32 = jnp.float32
     params = functools.partial(pltpu.CompilerParams, vmem_limit_bytes=VMEM_LIMIT)
 
     shifted = couple_src - low_count
     owner = jnp.where(couple_src >= low_count, shifted // band_count, own_index)
-    remote = owner != own_index
-    slot = shifted % band_count
-    asks = remote[None] & (owner[None] == jnp.arange(band_size)[:, None, None])
+    slot = jnp.where(owner != own_index, shifted % band_count, 0)
+    asks = owner[None] == jnp.arange(band_size)[:, None, None]
     wanted = jnp.max(jnp.where(asks, slot[None], 0), axis=(1, 2))
+    wanted = jnp.broadcast_to(wanted[:, None, None], (band_size, 1, 128))
     asked = lax.all_to_all(wanted, "band", split_axis=0, concat_axis=0, tiled=True)
 
     y_band, send = pl.pallas_call(
@@ -314,33 +423,29 @@
     )(asked, rho_band, kprev_band)
     received = lax.all_to_all(send, "band", split_axis=0, concat_axis=0, tiled=True)
 
-    level = jnp.sum(
-        jnp.where(
-            couple_mode[:, :, None] == jnp.arange(modes)[None, None, :],
-            occupation[:, None, :],
-            0,
-        ),
-        axis=-1,
-    ).astype(f32)
-    strength = pick(couple_mode, coupling_mag)
-    cos_mode, sin_mode = jnp.cos(coupling_phase), jnp.sin(coupling_phase)
-    is_down = couple_dir == 1
-    amp_down = jnp.sqrt(level * strength)
-    alpha = jnp.where(
-        is_down, amp_down * pick(couple_mode, cos_mode), jnp.sqrt((level + 1.0) * strength)
-    )
-    beta = jnp.where(is_down, amp_down * pick(couple_mode, sin_mode), 0.0)
-    site = couple_mode // EXPS
-    live = couple_src >= 0
-    is_low = live & (couple_src < low_count)
-    position = jnp.where(couple_src < low_count, couple_src, low_count + slot)
-    marks = jnp.concatenate([jnp.full((1,), -1, jnp.int32), low_mode])
-    held = (pick(jnp.clip(couple_src, 0, low_count - 1), marks) == couple_mode).astype(f32)
-    alpha_low = jnp.sqrt((held + 1.0) * strength)
-    damping = jnp.dot(occupation.astype(f32), damping_rate, precision=highest)
-    low_n, (low_j, low_s, low_a) = compact(is_low, [couple_src, site, alpha_low])
-    near_n, near = compact(live & ~remote, [position, site, alpha, beta])
-    far_n, far = compact(live & remote, [owner, site, alpha, beta])
+    whole_row = (1, -1)
+    own = jnp.stack([own_index, jnp.int32(band_size)]).astype(jnp.int32)
+    ints, flts = pl.pallas_call(
+        functools.partial(prep_kernel, low_count),
+        in_specs=[smem] + [vmem] * 9,
+        out_specs=[vmem, vmem],
+        out_shape=[
+            jax.ShapeDtypeStruct((8,) + couple_src.shape, jnp.int32),
+            jax.ShapeDtypeStruct((7,) + couple_src.shape, f32),
+        ],
+        name="prep",
+    )(
+        own,
+        couple_src,
+        couple_mode,
+        couple_dir,
+        occupation,
+        coupling_mag.reshape(whole_row),
+        jnp.cos(coupling_phase).reshape(whole_row),
+        jnp.sin(coupling_phase).reshape(whole_row),
+        damping_rate.reshape(whole_row),
+        low_mode.reshape(whole_row),
+    )
 
     h_re, h_im = hamiltonian[0], hamiltonian[1]
     left = jnp.block([[h_re, -h_im], [h_im, h_re]])
@@ -348,30 +453,17 @@
     col, row = state_site[:, None], state_site[None, :]
 
     turns = -(-low_count // band_size)
-    own_op = own_index + band_size * jnp.arange(turns, dtype=jnp.int32)
-    own_here = own_op < low_count
-    own_op = jnp.minimum(own_op, low_count - 1)
-    own_mode = pick(jnp.maximum(own_op - 1, 0), low_mode)
-    raised = (own_op >= 1).astype(f32)
-    own_amp = jnp.sqrt(pick(own_mode, coupling_mag)) * raised
-    own_int = jnp.stack([own_here.astype(jnp.int32), own_mode // EXPS], axis=1)
-    own_flt = jnp.stack(
-        [
-            pick(own_mode, damping_rate) * raised,
-            own_amp,
-            own_amp * pick(own_mode, cos_mode),
-            own_amp * pick(own_mode, sin_mode),
-        ],
-        axis=1,
+    own_op = jnp.minimum(
+        own_index + band_size * jnp.arange(turns, dtype=jnp.int32), low_count - 1
     )
     own_block = pl.BlockSpec((2, 1, size, size), lambda g, ops: (0, ops[g], 0, 0))
     top_block = pl.BlockSpec((2, 1, size, size), lambda g, ops: (0, 0, 0, 0))
     partial = pl.pallas_call(
-        low_kernel,
+        lambda ops, *refs: low_kernel(*refs),
         grid_spec=pltpu.PrefetchScalarGridSpec(
             num_scalar_prefetch=1,
             grid=(turns,),
-            in_specs=[smem] * 6
+            in_specs=[smem] * 2
             + [vmem, own_block, own_block, top_block, top_block]
             + [vmem] * 4,
             out_specs=vmem,
@@ -382,12 +474,8 @@
         name="low",
     )(
         own_op,
-        own_int,
-        own_flt,
-        low_n,
-        low_j,
-        low_s,
-        low_a,
+        ints,
+        flts,
         y_band,
         rho_low,
         kprev_low,
@@ -398,24 +486,25 @@
         col,
         row,
     )
-    k_low = lax.psum(partial, "band")
+    k_low = sum_over_band(partial.reshape(-1, size), band_size, own_index)
+    k_low = k_low.reshape(partial.shape)
 
     base = pl.pallas_call(
         local_kernel,
-        in_specs=[smem] * 6 + [vmem] * 7,
+        in_specs=[smem] * 2 + [vmem] * 7,
         out_specs=vmem,
         out_shape=jax.ShapeDtypeStruct((2, band_count, size, size), f32),
         scratch_shapes=[pltpu.VMEM((low_count + band_count, 2, size, size), f32)]
         + [pltpu.VMEM((sites, size, size), f32)] * 2,
         compiler_params=params(),
         name="local",
-    )(near_n, *near, damping, y_band, rho_low, kprev_low, left, right, col, row)
+    )(ints, flts, y_band, rho_low, kprev_low, left, right, col, row)
 
     block = size // 2
     k_band = pl.pallas_call(
         far_kernel,
         grid=(size // block,),
-        in_specs=[smem] * 5
+        in_specs=[smem] * 2
         + [
             pl.BlockSpec((band_size, 2, block, size), lambda g: (0, 0, g, 0)),
             pl.BlockSpec((2, band_count, block, size), lambda g: (0, 0, g, 0)),
@@ -427,7 +516,7 @@
         scratch_shapes=[pltpu.VMEM((sites, block, size), f32)] * 2,
         compiler_params=params(),
         name="far",
-    )(far_n, *far, received, base, col, row)
+    )(ints, flts, received, base, col, row)
     return (k_low, k_band)
 
 

time: 256 us -> 312 us (1.22)
  waiting for transfers between devices: 150 us -> 177 us
  starting transfers between devices: 3.76 us -> 27.2 us
  local copies, waits for them, and re-layouts: 5.63 us -> 27.9 us
  between operations: 19 us -> 0.77 us
  blocking collectives: 14.3 us -> 0 us
  Pallas kernels: 47.5 us -> 56.1 us
  other arithmetic: 14.3 us -> 21.7 us
    ppermute x0 -> x20, waiting for transfers between devices: none -> 177 us  [swap(): return lax.ppermute(x, 'band', pairs)]
    psum x1 -> x0, waiting for transfers between devices: 80.3 us -> none  [shards(): k_low = lax.psum(partial, 'band')]
    all_to_all x1, waiting for transfers between devices: 70 us -> 0.01 us  [shards(): lax.all_to_all(send, 'band', split_axis=0, concat_axis=0, tiled=True)]
    dynamic_slice x0 -> x15, local copies, waits for them, and re-layouts: none -> 19.2 us  [the longest x10 14.1 us: sum_over_band(): lax.dynamic_slice_in_dim(rows, start, length)]
    ppermute x0 -> x20, starting transfers between devices: none -> 15.2 us  [swap(): return lax.ppermute(x, 'band', pairs)]
    all_to_all x1 -> x0, blocking collectives: 14.3 us -> none  [shards(): lax.all_to_all(wanted, 'band', split_axis=0, concat_axis=0, tiled=True)]
    reduce_sum x12 -> x0, other arithmetic: 10.1 us -> none  [the longest x5 4.09 us: pick(): return jnp.sum(jnp.where(hit, table, 0), axis=-1).astype(table.dtype)]
    dynamic_slice x0 -> x5, other arithmetic: none -> 9.69 us  [sum_over_band(): give = lax.dynamic_slice_in_dim(rows, start + (1 - mine) * length, length)]
  transfers between devices with their start and end apart: 2 -> 22, of which waited for: 2 -> 19; matrix products, arithmetic and copies ran while one was open for 5% -> 11% of each run, Pallas kernels for 16% -> 9%
where the time goes in v2:
time: 312 us; the launch traced here: 311 us
  waiting for transfers between devices  177 us (57%)
  Pallas kernels  56.1 us (18%)
  local copies, waits for them, and re-layouts  27.9 us (9%)
  starting transfers between devices  27.2 us (9%)
  other arithmetic  21.7 us (7%)
    ppermute x20, waiting for transfers between devices, swap(): return lax.ppermute(x, 'band', pairs)  177 us
    pallas_call x1, Pallas kernels, shards(): pl.pallas_call(local_kernel, in_specs=[smem] * 2 + [vmem] * 7, out_specs=...  21.3 us
    ppermute x20, starting transfers between devices, swap(): return lax.ppermute(x, 'band', pairs)  15.2 us
    dynamic_slice x10, local copies, waits for them, and re-layouts, sum_over_band(): lax.dynamic_slice_in_dim(rows, start, length)  14.1 us
    pallas_call x1, Pallas kernels, shards(): pl.pallas_call(far_kernel, grid=(size // block,), in_specs=[smem] * 2 + [...  13.6 us
    dynamic_slice x5, other arithmetic, sum_over_band(): give = lax.dynamic_slice_in_dim(rows, start + (1 - mine) * length, length)  9.69 us
    dynamic_update_slice x5, other arithmetic, sum_over_band(): rows = lax.dynamic_update_slice_in_dim(rows, held + other, start, 0)  8.92 us
    pallas_call x1, Pallas kernels, shards(): pl.pallas_call(lambda ops, *refs: low_kernel(*refs), grid_spec=pltpu.Pref...  8.87 us
  transfers between devices with their start and end apart: 22, of which 19 were waited for; matrix products, arithmetic and copies ran while one was open for 11% of the time, Pallas kernels for 9%

profile of v2, /device:TPU:0, one launch (start us, length us, event | category | flops | bytes accessed | tf_op | source)
XLA Modules:
  0.0 310.7 jit_solution(2746895553884820468)
XLA Ops:
  2.2 7.3 %all-to-all-start = ((s32[32,1,128]{2,1,0:T(1,128)}), s32[32,1,128]{2,1,0:T(1,128)S(1)}, u32[]{:S(2)}, u32[]{:S(2)}) async-start(s32[32,1,128]{2,1,0:T(1,128)} %broadcast_in_dim.36), calls=%async_computation | async-start | bytes 32768 | tf_op jit(solution)/shard_map/all_to_all | solution.py:410
  15.4 6.2 %prep.1 = (s32[8,16,16]{2,1,0:T(8,128)}, f32[7,16,16]{2,1,0:T(8,128)}) custom-call(s32[2]{0:T(128)} %pad_add_fusion.own, s32[16,16]{1,0:T(8,128)} %src.1, s32[16,16]{1,0:T(8,128)} %mode.1, s32[16,16]{1,0:T(8,128)} %direction.1, s32[16,72]{1,0:T(8,128)} %occ.1, f32[1,72]{1,0:T(1,128)} %bitcast.25, f32[1,72]{1,0:T(1,128)} %get-tuple-element.37.cos, ...), custom_call_target="tpu_custom_call" | custom-call | tf_op jit(solution)/shard_map/prep/pallas_call | solution.py:428
  22.2 6.2 %send.1 = (f32[16,2,128,128]{3,2,1,0:T(8,128)}, f32[32,2,128,128]{3,2,1,0:T(8,128)}) custom-call(s32[32,1,128]{2,1,0:T(1,128)} %copy-done, f32[2,16,128,128]{3,2,1,0:T(8,128)} %rho.1, f32[2,16,128,128]{3,2,1,0:T(8,128)} %kprev.1), custom_call_target="tpu_custom_call" | custom-call | tf_op jit(solution)/shard_map/send/pallas_call | solution.py:412
  28.4 8.9 %low.1 = f32[2,32,128,128]{3,2,1,0:T(8,128)} custom-call(s32[1]{0:T(128)S(6)} %min.3.ops, s32[8,16,16]{2,1,0:T(8,128)} %get-tuple-element.6.refs_0_.ints, f32[7,16,16]{2,1,0:T(8,128)} %get-tuple-element.7.refs_1_.flts, f32[16,2,128,128]{3,2,1,0:T(8,128)} %get-tuple-element.8.refs_2_.y_band, f32[2,32,128,128]{3,2,1,0:T(8,128)} %rho_low.1, ...), custom_call_target="tpu_custom_call" | custom-call | tf_op jit(solution)/shard_map/low/pallas_call | solution.py:461
  41.3 2.7 constant_dynamic-slice_fusion.18
  52.0 12.2 %collective-permute-done.2 = f32[1024,128]{1,0:T(8,128)S(1)} collective-permute-done((f32[1024,128]{1,0:T(8,128)S(1)}, f32[1024,128]{1,0:T(8,128)S(1)}, u32[]{:S(2)}, u32[]{:S(2)}) %collective-permute-start.2) | collective-permute-done | bytes 524320 | tf_op jit(solution)/shard_map/ppermute | solution.py:350
  67.9 11.7 %collective-permute-done.3 = f32[1024,128]{1,0:T(8,128)S(1)} collective-permute-done((f32[1024,128]{1,0:T(8,128)S(1)}, f32[1024,128]{1,0:T(8,128)S(1)}, u32[]{:S(2)}, u32[]{:S(2)}) %collective-permute-start.3) | collective-permute-done | bytes 524320 | tf_op jit(solution)/shard_map/ppermute | solution.py:350
  83.9 5.5 %collective-permute-done.4 = f32[512,128]{1,0:T(8,128)S(1)} collective-permute-done((f32[512,128]{1,0:T(8,128)S(1)}, f32[512,128]{1,0:T(8,128)S(1)}, u32[]{:S(2)}, u32[]{:S(2)}) %collective-permute-start.4) | collective-permute-done | bytes 262176 | tf_op jit(solution)/shard_map/ppermute | solution.py:350
  92.5 4.7 %all-to-all-start.1 = ((f32[32,2,128,128]{3,2,1,0:T(8,128)}), f32[32,2,128,128]{3,2,1,0:T(8,128)}, u32[]{:S(2)}, u32[]{:S(2)}) async-start(f32[32,2,128,128]{3,2,1,0:T(8,128)} %get-tuple-element.9), calls=%async_computation.1 | async-start | bytes 8388608 | tf_op jit(solution)/shard_map/all_to_all | solution.py:424
  101.6 67.6 %collective-permute-done.6 = f32[256,128]{1,0:T(8,128)S(1)} collective-permute-done((f32[256,128]{1,0:T(8,128)S(1)}, f32[256,128]{1,0:T(8,128)S(1)}, u32[]{:S(2)}, u32[]{:S(2)}) %collective-permute-start.6) | collective-permute-done | bytes 131104 | tf_op jit(solution)/shard_map/ppermute | solution.py:350
  173.3 7.0 %collective-permute-done.7 = f32[256,128]{1,0:T(8,128)S(1)} collective-permute-done((f32[256,128]{1,0:T(8,128)S(1)}, f32[256,128]{1,0:T(8,128)S(1)}, u32[]{:S(2)}, u32[]{:S(2)}) %collective-permute-start.7) | collective-permute-done | bytes 131104 | tf_op jit(solution)/shard_map/ppermute | solution.py:350
  183.9 9.7 %collective-permute-done.8 = f32[128,128]{1,0:T(8,128)S(1)} collective-permute-done((f32[128,128]{1,0:T(8,128)S(1)}, f32[128,128]{1,0:T(8,128)S(1)}, u32[]{:S(2)}, u32[]{:S(2)}) %collective-permute-start.8) | collective-permute-done | bytes 65568 | tf_op jit(solution)/shard_map/ppermute | solution.py:350
  195.1 5.8 %collective-permute-done.9 = f32[128,128]{1,0:T(8,128)S(1)} collective-permute-done((f32[128,128]{1,0:T(8,128)S(1)}, f32[128,128]{1,0:T(8,128)S(1)}, u32[]{:S(2)}, u32[]{:S(2)}) %collective-permute-start.9) | collective-permute-done | bytes 65568 | tf_op jit(solution)/shard_map/ppermute | solution.py:350
  203.3 5.4 %collective-permute-done.10 = f32[128,128]{1,0:T(8,128)S(1)} collective-permute-done((f32[128,128]{1,0:T(8,128)S(1)}, f32[128,128]{1,0:T(8,128)S(1)}, u32[]{:S(2)}, u32[]{:S(2)}) %collective-permute-start.10) | collective-permute-done | bytes 65568 | tf_op jit(solution)/shard_map/ppermute | solution.py:350
  210.2 5.3 %collective-permute-done.11 = f32[128,128]{1,0:T(8,128)S(1)} collective-permute-done((f32[128,128]{1,0:T(8,128)S(1)}, f32[128,128]{1,0:T(8,128)S(1)}, u32[]{:S(2)}, u32[]{:S(2)}) %collective-permute-start.11) | collective-permute-done | bytes 65568 | tf_op jit(solution)/shard_map/ppermute | solution.py:350
  217.1 5.0 %collective-permute-done.12 = f32[256,128]{1,0:T(8,128)S(1)} collective-permute-done((f32[256,128]{1,0:T(8,128)S(1)}, f32[256,128]{1,0:T(8,128)S(1)}, u32[]{:S(2)}, u32[]{:S(2)}) %collective-permute-start.12) | collective-permute-done | bytes 131104 | tf_op jit(solution)/shard_map/ppermute | solution.py:350
  223.8 4.7 %collective-permute-done.13 = f32[256,128]{1,0:T(8,128)S(1)} collective-permute-done((f32[256,128]{1,0:T(8,128)S(1)}, f32[256,128]{1,0:T(8,128)S(1)}, u32[]{:S(2)}, u32[]{:S(2)}) %collective-permute-start.13) | collective-permute-done | bytes 131104 | tf_op jit(solution)/shard_map/ppermute | solution.py:350
  230.7 5.9 %collective-permute-done.14 = f32[512,128]{1,0:T(8,128)S(1)} collective-permute-done((f32[512,128]{1,0:T(8,128)S(1)}, f32[512,128]{1,0:T(8,128)S(1)}, u32[]{:S(2)}, u32[]{:S(2)}) %collective-permute-start.14) | collective-permute-done | bytes 262176 | tf_op jit(solution)/shard_map/ppermute | solution.py:350
  239.4 6.0 %collective-permute-done.15 = f32[512,128]{1,0:T(8,128)S(1)} collective-permute-done((f32[512,128]{1,0:T(8,128)S(1)}, f32[512,128]{1,0:T(8,128)S(1)}, u32[]{:S(2)}, u32[]{:S(2)}) %collective-permute-start.15) | collective-permute-done | bytes 262176 | tf_op jit(solution)/shard_map/ppermute | solution.py:350
  247.6 8.8 %collective-permute-done.16 = f32[1024,128]{1,0:T(8,128)S(1)} collective-permute-done((f32[1024,128]{1,0:T(8,128)S(1)}, f32[1024,128]{1,0:T(8,128)S(1)}, u32[]{:S(2)}, u32[]{:S(2)}) %collective-permute-start.16) | collective-permute-done | bytes 524320 | tf_op jit(solution)/shard_map/ppermute | solution.py:350
  258.9 8.6 %collective-permute-done.17 = f32[1024,128]{1,0:T(8,128)S(1)} collective-permute-done((f32[1024,128]{1,0:T(8,128)S(1)}, f32[1024,128]{1,0:T(8,128)S(1)}, u32[]{:S(2)}, u32[]{:S(2)}) %collective-permute-start.17) | collective-permute-done | bytes 524320 | tf_op jit(solution)/shard_map/ppermute | solution.py:350
  269.7 2.6 collective-permute-done.18
  274.8 21.3 %local.1.base = f32[2,16,128,128]{3,2,1,0:T(8,128)} custom-call(s32[8,16,16]{2,1,0:T(8,128)} %get-tuple-element.6.refs_0_.ints, f32[7,16,16]{2,1,0:T(8,128)} %get-tuple-element.7.refs_1_.flts, f32[16,2,128,128]{3,2,1,0:T(8,128)} %get-tuple-element.8.refs_2_.y_band, f32[2,32,128,128]{3,2,1,0:T(8,128)} %rho_low.1, f32[2,32,128,128]{3,2,1,0:T(8,128)} %kprev_low.1, ...), custom_call_target="tpu_custom_call" | custom-call | tf_op jit(solution)/shard_map/local/pallas_call | solution.py:492
  297.1 13.6 %far.1 = f32[2,16,128,128]{3,2,1,0:T(8,128)} custom-call(s32[8,16,16]{2,1,0:T(8,128)} %get-tuple-element.6.refs_0_.ints, f32[7,16,16]{2,1,0:T(8,128)} %get-tuple-element.7.refs_1_.flts, f32[32,2,128,128]{3,2,1,0:T(8,128)} %all-to-all-done.1.received, f32[2,16,128,128]{3,2,1,0:T(8,128)} %local.1.base, s32[128,1]{1,0:T(8,128)} %copy.19.refs_9_.col, ...), custom_call_target="tpu_custom_call" | custom-call | tf_op jit(solution)/shard_map/far/pallas_call | solution.py:504
  (66 shorter events, 67.3 us)
Async XLA Ops:
  2.2 19.4 %all-to-all-start = ((s32[32,1,128]{2,1,0:T(1,128)}), s32[32,1,128]{2,1,0:T(1,128)S(1)}, u32[]{:S(2)}, u32[]{:S(2)}) async-start(s32[32,1,128]{2,1,0:T(1,128)} %broadcast_in_dim.36), calls=%async_computation | async-start | bytes 32768 | tf_op jit(solution)/shard_map/all_to_all | solution.py:410
  21.6 0.6 copy-start
  38.5 2.7 collective-permute-start
  43.9 2.7 collective-permute-start.1
  50.0 14.3 %collective-permute-start.2 = (f32[1024,128]{1,0:T(8,128)S(1)}, f32[1024,128]{1,0:T(8,128)S(1)}, u32[]{:S(2)}, u32[]{:S(2)}) collective-permute-start(f32[1024,128]{1,0:T(8,128)S(1)} %constant_dynamic-slice_fusion.16), channel_id=1, source_target_pairs={{0,2},{1,3},{2,0},{3,1},{4,6},{5,7},{6,4},{7,5},{8,10},{9,11},{10,... | collective-permute-start | bytes 1572872 | tf_op jit(solution)/shard_map/ppermute | solution.py:350
  66.3 13.3 %collective-permute-start.3 = (f32[1024,128]{1,0:T(8,128)S(1)}, f32[1024,128]{1,0:T(8,128)S(1)}, u32[]{:S(2)}, u32[]{:S(2)}) collective-permute-start(f32[1024,128]{1,0:T(8,128)S(1)} %get-tuple-element.26), channel_id=1, source_target_pairs={{0,4},{1,5},{2,6},{3,7},{4,0},{5,1},{6,2},{7,3},{8,12},{9,13},{10,... | collective-permute-start | bytes 1572872 | tf_op jit(solution)/shard_map/ppermute | solution.py:350
  82.5 6.9 %collective-permute-start.4 = (f32[512,128]{1,0:T(8,128)S(1)}, f32[512,128]{1,0:T(8,128)S(1)}, u32[]{:S(2)}, u32[]{:S(2)}) collective-permute-start(f32[512,128]{1,0:T(8,128)S(1)} %constant_dynamic-slice_fusion.13), channel_id=1, source_target_pairs={{0,4},{1,5},{2,6},{3,7},{4,0},{5,1},{6,2},{7,3},{8,12},{9,13},{10,... | collective-permute-start | bytes 786440 | tf_op jit(solution)/shard_map/ppermute | solution.py:350
  91.2 6.4 %collective-permute-start.5 = (f32[512,128]{1,0:T(8,128)S(1)}, f32[512,128]{1,0:T(8,128)S(1)}, u32[]{:S(2)}, u32[]{:S(2)}) collective-permute-start(f32[512,128]{1,0:T(8,128)S(1)} %get-tuple-element.24), channel_id=1, source_target_pairs={{0,2},{1,3},{2,0},{3,1},{4,6},{5,7},{6,4},{7,5},{8,10},{9,11},{10,... | collective-permute-start | bytes 786440 | tf_op jit(solution)/shard_map/ppermute | solution.py:350
  92.5 204.6 %all-to-all-start.1 = ((f32[32,2,128,128]{3,2,1,0:T(8,128)}), f32[32,2,128,128]{3,2,1,0:T(8,128)}, u32[]{:S(2)}, u32[]{:S(2)}) async-start(f32[32,2,128,128]{3,2,1,0:T(8,128)} %get-tuple-element.9), calls=%async_computation.1 | async-start | bytes 8388608 | tf_op jit(solution)/shard_map/all_to_all | solution.py:424
  100.2 69.0 %collective-permute-start.6 = (f32[256,128]{1,0:T(8,128)S(1)}, f32[256,128]{1,0:T(8,128)S(1)}, u32[]{:S(2)}, u32[]{:S(2)}) collective-permute-start(f32[256,128]{1,0:T(8,128)S(1)} %constant_dynamic-slice_fusion.10), channel_id=1, source_target_pairs={{0,8},{1,9},{2,10},{3,11},{4,12},{5,13},{6,14},{7,15},{8,0},{9,1},... | collective-permute-start | bytes 393224 | tf_op jit(solution)/shard_map/ppermute | solution.py:350
  170.8 9.5 %collective-permute-start.7 = (f32[256,128]{1,0:T(8,128)S(1)}, f32[256,128]{1,0:T(8,128)S(1)}, u32[]{:S(2)}, u32[]{:S(2)}) collective-permute-start(f32[256,128]{1,0:T(8,128)S(1)} %get-tuple-element.22), channel_id=1, source_target_pairs={{0,8},{1,9},{2,10},{3,11},{4,12},{5,13},{6,14},{7,15},{8,0},{9,1},... | collective-permute-start | bytes 393224 | tf_op jit(solution)/shard_map/ppermute | solution.py:350
  182.7 10.9 %collective-permute-start.8 = (f32[128,128]{1,0:T(8,128)S(1)}, f32[128,128]{1,0:T(8,128)S(1)}, u32[]{:S(2)}, u32[]{:S(2)}) collective-permute-start(f32[128,128]{1,0:T(8,128)S(1)} %constant_dynamic-slice_fusion.7), channel_id=1, source_target_pairs={{0,16},{1,17},{2,18},{3,19},{4,20},{5,21},{6,22},{7,23},{8,24},{9,... | collective-permute-start | bytes 196616 | tf_op jit(solution)/shard_map/ppermute | solution.py:350
  195.1 5.8 %collective-permute-start.9 = (f32[128,128]{1,0:T(8,128)S(1)}, f32[128,128]{1,0:T(8,128)S(1)}, u32[]{:S(2)}, u32[]{:S(2)}) collective-permute-start(f32[128,128]{1,0:T(8,128)S(1)} %get-tuple-element.20), channel_id=1, source_target_pairs={{0,16},{1,17},{2,18},{3,19},{4,20},{5,21},{6,22},{7,23},{8,24},{9,... | collective-permute-start | bytes 196616 | tf_op jit(solution)/shard_map/ppermute | solution.py:350
  203.3 5.4 %collective-permute-start.10 = (f32[128,128]{1,0:T(8,128)S(1)}, f32[128,128]{1,0:T(8,128)S(1)}, u32[]{:S(2)}, u32[]{:S(2)}) collective-permute-start(f32[128,128]{1,0:T(8,128)S(1)} %constant_dynamic-slice_fusion.5), channel_id=1, source_target_pairs={{0,16},{1,17},{2,18},{3,19},{4,20},{5,21},{6,22},{7,23},{8,24},{9,... | collective-permute-start | bytes 196616 | tf_op jit(solution)/shard_map/ppermute | solution.py:350
  210.2 5.3 %collective-permute-start.11 = (f32[128,128]{1,0:T(8,128)S(1)}, f32[128,128]{1,0:T(8,128)S(1)}, u32[]{:S(2)}, u32[]{:S(2)}) collective-permute-start(f32[128,128]{1,0:T(8,128)S(1)} %get-tuple-element.18), channel_id=1, source_target_pairs={{0,16},{1,17},{2,18},{3,19},{4,20},{5,21},{6,22},{7,23},{8,24},{9,... | collective-permute-start | bytes 196616 | tf_op jit(solution)/shard_map/ppermute | solution.py:350
  217.0 5.0 %collective-permute-start.12 = (f32[256,128]{1,0:T(8,128)S(1)}, f32[256,128]{1,0:T(8,128)S(1)}, u32[]{:S(2)}, u32[]{:S(2)}) collective-permute-start(f32[256,128]{1,0:T(8,128)S(1)} %constant_dynamic-slice_fusion.3), channel_id=1, source_target_pairs={{0,8},{1,9},{2,10},{3,11},{4,12},{5,13},{6,14},{7,15},{8,0},{9,1},... | collective-permute-start | bytes 393224 | tf_op jit(solution)/shard_map/ppermute | solution.py:350
  223.6 5.0 %collective-permute-start.13 = (f32[256,128]{1,0:T(8,128)S(1)}, f32[256,128]{1,0:T(8,128)S(1)}, u32[]{:S(2)}, u32[]{:S(2)}) collective-permute-start(f32[256,128]{1,0:T(8,128)S(1)} %get-tuple-element.16), channel_id=1, source_target_pairs={{0,8},{1,9},{2,10},{3,11},{4,12},{5,13},{6,14},{7,15},{8,0},{9,1},... | collective-permute-start | bytes 393224 | tf_op jit(solution)/shard_map/ppermute | solution.py:350
  230.2 6.4 %collective-permute-start.14 = (f32[512,128]{1,0:T(8,128)S(1)}, f32[512,128]{1,0:T(8,128)S(1)}, u32[]{:S(2)}, u32[]{:S(2)}) collective-permute-start(f32[512,128]{1,0:T(8,128)S(1)} %constant_dynamic-slice_fusion.1), channel_id=1, source_target_pairs={{0,4},{1,5},{2,6},{3,7},{4,0},{5,1},{6,2},{7,3},{8,12},{9,13},{10,... | collective-permute-start | bytes 786440 | tf_op jit(solution)/shard_map/ppermute | solution.py:350
  238.4 7.0 %collective-permute-start.15 = (f32[512,128]{1,0:T(8,128)S(1)}, f32[512,128]{1,0:T(8,128)S(1)}, u32[]{:S(2)}, u32[]{:S(2)}) collective-permute-start(f32[512,128]{1,0:T(8,128)S(1)} %get-tuple-element.14), channel_id=1, source_target_pairs={{0,2},{1,3},{2,0},{3,1},{4,6},{5,7},{6,4},{7,5},{8,10},{9,11},{10,... | collective-permute-start | bytes 786440 | tf_op jit(solution)/shard_map/ppermute | solution.py:350
  247.2 9.2 %collective-permute-start.16 = (f32[1024,128]{1,0:T(8,128)S(1)}, f32[1024,128]{1,0:T(8,128)S(1)}, u32[]{:S(2)}, u32[]{:S(2)}) collective-permute-start(f32[1024,128]{1,0:T(8,128)S(1)} %constant_dynamic-slice_fusion.8), channel_id=1, source_target_pairs={{0,2},{1,3},{2,0},{3,1},{4,6},{5,7},{6,4},{7,5},{8,10},{9,11},{10,... | collective-permute-start | bytes 1572872 | tf_op jit(solution)/shard_map/ppermute | solution.py:350
  258.3 9.2 %collective-permute-start.17 = (f32[1024,128]{1,0:T(8,128)S(1)}, f32[1024,128]{1,0:T(8,128)S(1)}, u32[]{:S(2)}, u32[]{:S(2)}) collective-permute-start(f32[1024,128]{1,0:T(8,128)S(1)} %get-tuple-element.12), channel_id=1, source_target_pairs={{0,4},{1,5},{2,6},{3,7},{4,0},{5,1},{6,2},{7,3},{8,12},{9,13},{10,... | collective-permute-start | bytes 1572872 | tf_op jit(solution)/shard_map/ppermute | solution.py:350
  269.6 2.7 collective-permute-start.18
  274.7 21.4 %collective-permute-start.19 = (f32[2048,128]{1,0:T(8,128)S(1)}, f32[2048,128]{1,0:T(8,128)S(1)}, u32[]{:S(2)}, u32[]{:S(2)}) collective-permute-start(f32[2048,128]{1,0:T(8,128)S(1)} %get-tuple-element.10), channel_id=1, source_target_pairs={{0,1},{1,0},{2,3},{3,2},{4,5},{5,4},{6,7},{7,6},{8,9},{9,8},{10,11... | collective-permute-start | bytes 3145736 | tf_op jit(solution)/shard_map/ppermute | solution.py:350
